TPU v7x, 32 devices: a whole 2x2x4 slice. The times are simulated.
32 devices in a mesh: real: 4 (over y, core), sky: 8 (over z, x).
Axes of the slice: x: 2, y: 2, z: 4, core: 2. Of those that a mesh axis runs over, the one named last changes fastest.
Arguments:
- potential_stock: bfloat16 [8, 256, 16384], P('real', 'sky'), may hold values from -6 to 6
- plane_pick: int32 [4], replicated, may hold values from 0 to 7, as said below
- col_shift: int32 [4, 4], P('real'), may hold values from 0 to 16383
- mirror: int32 [4, 4], P('real'), may hold values from 0 to 1
- subcell: int32 [32, 16], P('sky'), may hold values from 0 to 15
- lens_weight: float32 [4], replicated, may hold values from 0.02 to 0.08
Outputs:
- deflect: float32 [2, 4, 256, 2048], P(None, 'real', 'sky')
- distort: float32 [4, 4, 256, 2048], P(None, 'real', 'sky')
Inputs may be any that keep to these rules, and one draw needn't show every extreme that they name: `plane_pick`: the 4 entries are distinct stored entries; entry q is held by the realization group q // 2.
All inputs are finite; a program needn't handle non-finite values.
Results may differ from a plain program's by a relative error of at most 0.0003.
Values may be sent and summed in bfloat16 or wider, within the bound.
A program may use at most 64 MiB of HBM per device.

v0:
```python
import jax
import jax.numpy as jnp
from jax import lax
from jax.sharding import PartitionSpec as P

PLANES = 4
SUB = 4
TILE_R = 8
TILE_C = 128
first_coef = (1.0 / 12.0, -8.0 / 12.0, 0.0, 8.0 / 12.0, -1.0 / 12.0)
second_coef = (-1.0 / 12.0, 16.0 / 12.0, -30.0 / 12.0, 16.0 / 12.0, -1.0 / 12.0)


def extended_2(x, sides, width):
    for axis, dim in sides:
        peers, length = (lax.axis_size(axis), x.shape[dim])
        up = [(i, (i + 1) % peers) for i in range(peers)]
        down = [(j, i) for i, j in up]
        last = lax.slice_in_dim(x, length - width, length, axis=dim)
        first = lax.slice_in_dim(x, 0, width, axis=dim)
        before = lax.ppermute(last, axis, up)
        after = lax.ppermute(first, axis, down)
        x = jnp.concatenate([before, x, after], axis=dim)
    return x


def spread(value, axis, source):
    kept = jnp.where(lax.axis_index(axis) == source, value, 0).astype(value.dtype)
    return lax.psum(kept, axis)


def cubic_weights(frac):
    sq = frac * frac
    cube = sq * frac
    return (
        (-cube + 2.0 * sq - frac) * 0.5,
        (3.0 * cube - 5.0 * sq + 2.0) * 0.5,
        (-3.0 * cube + 4.0 * sq + frac) * 0.5,
        (cube - sq) * 0.5,
    )


def tap_weights(subcell):
    frac_x = ((subcell % SUB).astype(jnp.float32) + 0.5) / SUB
    frac_y = ((subcell // SUB).astype(jnp.float32) + 0.5) / SUB
    weights_x = tuple((w[:, None, :, None] for w in cubic_weights(frac_x)))
    weights_y = tuple((w[:, None, :, None] for w in cubic_weights(frac_y)))
    return (weights_x, weights_y)


def derivatives(tile):
    nrows = tile.shape[0] - 5
    ncols = tile.shape[1] - 5

    def window(drow, dcol):
        return tile[3 + drow : 3 + drow + nrows, 3 + dcol : 3 + dcol + ncols]

    grad_x = sum((first_coef[q] * window(0, q - 2) for q in range(5) if q != 2))
    grad_y = sum((first_coef[q] * window(q - 2, 0) for q in range(5) if q != 2))
    hess_xx = sum((second_coef[q] * window(0, q - 2) for q in range(5)))
    hess_yy = sum((second_coef[q] * window(q - 2, 0) for q in range(5)))
    hess_xy = sum(
        (
            first_coef[p] * first_coef[q] * window(p - 2, q - 2)
            for p in range(5)
            for q in range(5)
            if p != 2 and q != 2
        )
    )
    return (grad_x, grad_y, hess_xx, hess_yy, hess_xy)


def sample(field, weights_x, weights_y, nrows, ncols):
    total = jnp.zeros((nrows // TILE_R, TILE_R, ncols // TILE_C, TILE_C), jnp.float32)
    for brow in range(4):
        inner = jnp.zeros_like(total)
        for acol in range(4):
            piece = field[brow : brow + nrows, acol : acol + ncols]
            piece = piece.reshape(nrows // TILE_R, TILE_R, ncols // TILE_C, TILE_C)
            inner = inner + weights_x[acol] * piece
        total = total + weights_y[brow] * inner
    return total.reshape(nrows, ncols)


def advance(state, tile, weights_x, weights_y, lens):
    nrows = tile.shape[0] - 8
    ncols = tile.shape[1] - 8
    fields = derivatives(tile.astype(jnp.float32))
    grad_x, grad_y, hess_xx, hess_yy, hess_xy = [
        sample(f, weights_x, weights_y, nrows, ncols) for f in fields
    ]
    shift_x, shift_y, a_11, a_12, a_21, a_22 = state
    shift_x = shift_x + lens * grad_x
    shift_y = shift_y + lens * grad_y
    new_11 = a_11 - lens * (hess_xx * a_11 + hess_xy * a_21)
    new_12 = a_12 - lens * (hess_xx * a_12 + hess_xy * a_22)
    new_21 = a_21 - lens * (hess_xy * a_11 + hess_yy * a_21)
    new_22 = a_22 - lens * (hess_xy * a_12 + hess_yy * a_22)
    return (shift_x, shift_y, new_11, new_12, new_21, new_22)


def cut_columns(band, shift, flip, width):
    flipped = jnp.where(flip == 1, band[..., ::-1], band)
    extended = jnp.concatenate([flipped, flipped[..., : width + 8]], axis=-1)
    start = (shift - 4) % band.shape[-1]
    return lax.dynamic_slice_in_dim(extended, start, width + 8, flipped.ndim - 1)


def add_edges(blocks):
    return extended_2(blocks, (("sky", 1),), 4)


def body(potential_stock, plane_pick, col_shift, mirror, subcell, lens_weight):
    nrows = subcell.shape[0] * TILE_R
    ncols = subcell.shape[1] * TILE_C
    held = potential_stock.shape[0]
    weights_x, weights_y = tap_weights(subcell)
    zeros = jnp.zeros((nrows, ncols), jnp.float32)
    ones = jnp.ones((nrows, ncols), jnp.float32)
    state = (zeros, zeros, ones, zeros, zeros, ones)
    for plane in range(PLANES):
        entry = plane_pick[plane]
        own = lax.dynamic_index_in_dim(potential_stock, entry % held, 0, keepdims=False)
        band = spread(own, "real", entry // held)
        view = add_edges(cut_columns(band, col_shift[0, plane], mirror[0, plane], ncols)[None])[0]
        state = advance(state, view, weights_x, weights_y, lens_weight[plane])
    deflect = jnp.stack([state[0], state[1]])[:, None]
    distort = jnp.stack([state[2], state[3], state[4], state[5]])[:, None]
    return (deflect, distort)


def solution(mesh):
    return jax.shard_map(
        body,
        mesh=mesh,
        in_specs=(
            P("real", "sky", None),
            P(),
            P("real", None),
            P("real", None),
            P("sky", None),
            P(),
        ),
        out_specs=(P(None, "real", "sky", None), P(None, "real", "sky", None)),
        check_vma=False,
    )
```

profile of v0, /device:TPU:0, one launch (start us, length us, event | category | flops | bytes accessed | tf_op | source)
XLA Modules:
  0.0 336.1 jit_solution(15241077179185360147)
XLA Ops:
  7.2 1.4 fusion.436
  18.8 4.3 %select_bitcast_fusion.3 = (bf16[32,16384]{1,0:T(8,128)(2,1)}, bf16[32,16384]{1,0:T(8,128)(2,1)}, bf16[32,16384]{1,0:T(8,128)(2,1)}, bf16[32,16384]{1,0:T(8,128)(2,1)}) fusion(bf16[2,32,16384]{2,1,0:T(8,128)(2,1)} %param.6, s32[]{:T(128)S(6)} %select_n.154, pred[]{:T(512)S(6)} %eq.49, s32[]{:T(128)S(6)} %select_n.164, pred[]{:T(512)S(6)} %eq.52, ...), kind=kLoop, calls=%fused_computation.412 | loop fusion | flops 2097152 | bytes 8388628 | tf_op jit(solution)/shard_map/jit(_where)/select_n | solution.py:28
  23.1 0.6 copy-done.4
  23.7 0.7 fusion.435
  27.0 0.7 fusion.434
  30.2 0.7 fusion.433
  30.9 80.6 %all-reduce.3.cloned.1.call-done = (bf16[32,16384]{1,0:T(8,128)(2,1)}, bf16[32,16384]{1,0:T(8,128)(2,1)}, bf16[32,16384]{1,0:T(8,128)(2,1)}, bf16[32,16384]{1,0:T(8,128)(2,1)}) async-done(((bf16[32,16384]{1,0:T(8,128)(2,1)}, bf16[32,16384]{1,0:T(8,128)(2,1)}, bf16[32,16384]{1,0:T(8,128)(2,1)}, bf16[32,16384]{1,0:T(8,128)(2,1)}), (bf16[32,16384]{1,0:T(8,128)(2,1)}, bf16[32,16384]{1,0:T(8,128)(2,1)}, ...) | async-done | bytes 4194320 | tf_op jit(solution)/shard_map/psum | solution.py:29
  111.5 50.0 %rev.15 = bf16[32,16384]{1,0:T(8,128)(2,1)S(1)} reverse(bf16[32,16384]{1,0:T(8,128)(2,1)} %get-tuple-element.2), dimensions={1} | reverse | bytes 2097152 | tf_op jit(solution)/shard_map/rev | solution.py:103
  161.5 43.2 %rev.14 = bf16[32,16384]{1,0:T(8,128)(2,1)} reverse(bf16[32,16384]{1,0:T(8,128)(2,1)S(1)} %copy-done.3), dimensions={1} | reverse | bytes 2097152 | tf_op jit(solution)/shard_map/rev | solution.py:103
  204.8 1.4 broadcast_select_fusion
  206.2 0.2 fusion.387
  206.5 0.6 fusion.432
  207.1 4.2 %collective-permute-start.7 = (bf16[1,4,2056]{2,1,0:T(4,128)(2,1)}, bf16[1,4,2056]{2,1,0:T(4,128)(2,1)S(1)}, u32[]{:S(2)}, u32[]{:S(2)}) collective-permute-start(bf16[1,4,2056]{2,1,0:T(4,128)(2,1)} %get-tuple-element.60), channel_id=1, source_target_pairs={{1,0},{2,1},{3,2},{4,3},{5,4},{6,5},{7,6},{0,7},{9,8},{10,9},{11,1... | collective-permute-start | bytes 49352 | tf_op jit(solution)/shard_map/ppermute | solution.py:22
  211.3 0.2 fusion.386
  211.6 0.6 fusion.431
  212.2 4.7 %collective-permute-start.5 = (bf16[1,4,2056]{2,1,0:T(4,128)(2,1)}, bf16[1,4,2056]{2,1,0:T(4,128)(2,1)S(1)}, u32[]{:S(2)}, u32[]{:S(2)}) collective-permute-start(bf16[1,4,2056]{2,1,0:T(4,128)(2,1)} %get-tuple-element.58), channel_id=1, source_target_pairs={{1,0},{2,1},{3,2},{4,3},{5,4},{6,5},{7,6},{0,7},{9,8},{10,9},{11,1... | collective-permute-start | bytes 49352 | tf_op jit(solution)/shard_map/ppermute | solution.py:22
  216.9 10.6 %rev.13 = bf16[32,16384]{1,0:T(8,128)(2,1)S(1)} reverse(bf16[32,16384]{1,0:T(8,128)(2,1)S(1)} %copy-done), dimensions={1} | reverse | bytes 2097152 | tf_op jit(solution)/shard_map/rev | solution.py:103
  227.6 43.2 %rev.12 = bf16[32,16384]{1,0:T(8,128)(2,1)} reverse(bf16[32,16384]{1,0:T(8,128)(2,1)S(1)} %copy-done.1), dimensions={1} | reverse | bytes 2097152 | tf_op jit(solution)/shard_map/rev | solution.py:103
  270.8 1.4 broadcast_select_fusion.2
  272.3 0.2 fusion.384
  272.5 0.1 collective-permute-start.1
  272.6 2.0 collective-permute-start
  274.6 0.2 fusion.385
  274.9 1.5 collective-permute-done.1
  276.3 2.7 collective-permute-start.3
  279.2 0.9 add_add_fusion.7
  280.0 1.5 fusion.45
  281.6 0.4 collective-permute-start.4
  281.9 3.6 %collective-permute-done.2 = bf16[1,4,2056]{2,1,0:T(4,128)(2,1)S(1)} collective-permute-done((bf16[1,4,2056]{2,1,0:T(4,128)(2,1)S(1)}, bf16[1,4,2056]{2,1,0:T(4,128)(2,1)S(1)}, u32[]{:S(2)}, u32[]{:S(2)}) %collective-permute-start.2) | collective-permute-done | bytes 16480 | tf_op jit(solution)/shard_map/ppermute | solution.py:21
  285.5 0.1 fusion.377
  285.6 0.9 add_add_fusion.3
  286.5 1.5 fusion.30
  288.0 0.1 fusion.379
  288.1 0.9 add_add_fusion
  289.0 1.5 fusion
  290.5 0.9 add_add_fusion.1
  291.4 1.5 fusion.15
  292.9 6.8 %fusion.87 = f32[1,32,2048]{2,1,0:T(8,128)S(1)} fusion(f32[35,2051]{1,0:T(8,128)S(1)} %get-tuple-element.38, f32[35,2051]{1,0:T(8,128)S(1)} %get-tuple-element.42, f32[35,2051]{1,0:T(8,128)S(1)} %get-tuple-element.46, f32[35,2051]{1,0:T(8,128)S(1)} %get-tuple-element.50, f32[]{:T(128)} %bitcast.32, f32[]{:T(128)} %bitcast.24, f32[]{:T(128)} %bitcast.16, ...), kind=kLoop, calls=%fused_computation.597 | loop fusion | flops 9633792 | bytes 17041424 | tf_op jit(solution)/shard_map/stack | solution.py:127
  299.7 6.6 %fusion.67 = f32[1,32,2048]{2,1,0:T(8,128)S(1)} fusion(f32[35,2051]{1,0:T(8,128)S(1)} %get-tuple-element.39, f32[35,2051]{1,0:T(8,128)S(1)} %get-tuple-element.43, f32[35,2051]{1,0:T(8,128)S(1)} %get-tuple-element.47, f32[35,2051]{1,0:T(8,128)S(1)} %get-tuple-element.51, f32[]{:T(128)} %bitcast.32, f32[]{:T(128)} %bitcast.24, f32[]{:T(128)} %bitcast.16, ...), kind=kLoop, calls=%fused_computation.577 | loop fusion | flops 9633792 | bytes 17041424 | tf_op jit(solution)/shard_map/stack | solution.py:127
  306.3 0.8 maximum_bitcast_fusion.1
  307.2 6.1 %multiply_subtract_fusion.9 = (f32[32,2048]{1,0:T(8,128)S(1)}, f32[32,2048]{1,0:T(8,128)S(1)}, f32[32,2048]{1,0:T(8,128)S(1)}, f32[32,2048]{1,0:T(8,128)S(1)}, f...) fusion(f32[]{:T(128)} %bitcast.16, f32[]{:T(128)} %bitcast, f32[35,2051]{1,0:T(8,128)S(1)} %get-tuple-element.48, ...), kind=kLoop, calls=%fused_computation.899 | loop fusion | flops 12320768 | bytes 22546440 | tf_op jit(solution)/shard_map/sub | solution.py:95
  313.3 2.8 multiply_subtract_fusion.8
  316.1 1.4 multiply_subtract_fusion.2
  317.5 6.2 %subtract_bitcast_fusion.3 = (f32[1,32,2048]{2,1,0:T(8,128)S(1)}, f32[32,2048]{1,0:T(8,128)S(1)}, f32[32,2048]{1,0:T(8,128)S(1)}, f32[32,2048]{1,0:T(8,128)S(1)}...) fusion(f32[]{:T(128)} %bitcast.32, ...), kind=kLoop, calls=%fused_computation.895 | loop fusion | flops 12451840 | bytes 23595016 | tf_op jit(solution)/shard_map/stack | solution.py:128
  323.7 2.2 subtract_bitcast_fusion.1
  325.9 1.5 subtract_bitcast_fusion.2
  327.4 0.7 subtract_bitcast_fusion
  328.2 1.1 maximum_bitcast_fusion
  (35 shorter events, 0.4 us)
Async XLA Ops:
  7.2 104.3 %all-reduce.3.cloned.1.call-start = ((), (), s32[]{:S(2)}) async-start(), calls=%async_computation | async-start | bytes 8388608 | tf_op jit(solution)/shard_map/psum | solution.py:29
  23.0 0.7 copy-start.4
  23.0 4.0 %copy-start.5 = (s32[1,4]{1,0:T(1,128)S(1)}, s32[1,4]{1,0:T(1,128)}, u32[]{:S(2)}) copy-start(s32[1,4]{1,0:T(1,128)} %param.9) | copy-start | bytes 52
  23.0 7.2 %copy-start.6 = (f32[4]{0:T(128)S(1)}, f32[4]{0:T(128)}, u32[]{:S(2)}) copy-start(f32[4]{0:T(128)} %param.11) | copy-start | bytes 52
  23.0 7.9 %copy-start.7 = (s32[4,16]{1,0:T(4,128)S(1)}, s32[4,16]{1,0:T(4,128)}, u32[]{:S(2)}) copy-start(s32[4,16]{1,0:T(4,128)} %param.10) | copy-start | bytes 772
  111.5 50.0 %copy-start.3 = (bf16[32,16384]{1,0:T(8,128)(2,1)S(1)}, bf16[32,16384]{1,0:T(8,128)(2,1)}, u32[]{:S(2)}) copy-start(bf16[32,16384]{1,0:T(8,128)(2,1)} %get-tuple-element.3) | copy-start | bytes 3145732
  161.5 43.2 %copy-start.2 = (bf16[32,16384]{1,0:T(8,128)(2,1)S(1)}, bf16[32,16384]{1,0:T(8,128)(2,1)}, u32[]{:S(2)}) copy-start(bf16[32,16384]{1,0:T(8,128)(2,1)} %get-tuple-element.2) | copy-start | bytes 3145732
  206.4 10.5 %copy-start = (bf16[32,16384]{1,0:T(8,128)(2,1)S(1)}, bf16[32,16384]{1,0:T(8,128)(2,1)}, u32[]{:S(2)}) copy-start(bf16[32,16384]{1,0:T(8,128)(2,1)} %get-tuple-element.4) | copy-start | bytes 3145732
  207.1 80.9 %collective-permute-start.7 = (bf16[1,4,2056]{2,1,0:T(4,128)(2,1)}, bf16[1,4,2056]{2,1,0:T(4,128)(2,1)S(1)}, u32[]{:S(2)}, u32[]{:S(2)}) collective-permute-start(bf16[1,4,2056]{2,1,0:T(4,128)(2,1)} %get-tuple-element.60), channel_id=1, source_target_pairs={{1,0},{2,1},{3,2},{4,3},{5,4},{6,5},{7,6},{0,7},{9,8},{10,9},{11,1... | collective-permute-start | bytes 49352 | tf_op jit(solution)/shard_map/ppermute | solution.py:22
  211.3 76.7 %collective-permute-start.6 = (bf16[1,4,2056]{2,1,0:T(4,128)(2,1)}, bf16[1,4,2056]{2,1,0:T(4,128)(2,1)S(1)}, u32[]{:S(2)}, u32[]{:S(2)}) collective-permute-start(bf16[1,4,2056]{2,1,0:T(4,128)(2,1)} %get-tuple-element.59), channel_id=1, source_target_pairs={{0,1},{1,2},{2,3},{3,4},{4,5},{5,6},{6,7},{7,0},{8,9},{9,10},{10,1... | collective-permute-start | bytes 49352 | tf_op jit(solution)/shard_map/ppermute | solution.py:21
  211.6 16.0 %copy-start.1 = (bf16[32,16384]{1,0:T(8,128)(2,1)S(1)}, bf16[32,16384]{1,0:T(8,128)(2,1)}, u32[]{:S(2)}) copy-start(bf16[32,16384]{1,0:T(8,128)(2,1)} %get-tuple-element.5) | copy-start | bytes 3145732
  212.2 78.3 %collective-permute-start.5 = (bf16[1,4,2056]{2,1,0:T(4,128)(2,1)}, bf16[1,4,2056]{2,1,0:T(4,128)(2,1)S(1)}, u32[]{:S(2)}, u32[]{:S(2)}) collective-permute-start(bf16[1,4,2056]{2,1,0:T(4,128)(2,1)} %get-tuple-element.58), channel_id=1, source_target_pairs={{1,0},{2,1},{3,2},{4,3},{5,4},{6,5},{7,6},{0,7},{9,8},{10,9},{11,1... | collective-permute-start | bytes 49352 | tf_op jit(solution)/shard_map/ppermute | solution.py:22
  272.5 3.8 %collective-permute-start.1 = (bf16[1,4,2056]{2,1,0:T(4,128)(2,1)S(1)}, bf16[1,4,2056]{2,1,0:T(4,128)(2,1)S(1)}, u32[]{:S(2)}, u32[]{:S(2)}) collective-permute-start(bf16[1,4,2056]{2,1,0:T(4,128)(2,1)S(1)} %get-tuple-element.54), channel_id=1, source_target_pairs={{1,0},{2,1},{3,2},{4,3},{5,4},{6,5},{7,6},{0,7},{9,8},{10,9},{11,1... | collective-permute-start | bytes 49352 | tf_op jit(solution)/shard_map/ppermute | solution.py:22
  272.6 6.5 %collective-permute-start = (bf16[1,4,2056]{2,1,0:T(4,128)(2,1)S(1)}, bf16[1,4,2056]{2,1,0:T(4,128)(2,1)S(1)}, u32[]{:S(2)}, u32[]{:S(2)}) collective-permute-start(bf16[1,4,2056]{2,1,0:T(4,128)(2,1)S(1)} %get-tuple-element.53), channel_id=1, source_target_pairs={{0,1},{1,2},{2,3},{3,4},{4,5},{5,6},{6,7},{7,0},{8,9},{9,10},{10,1... | collective-permute-start | bytes 49352 | tf_op jit(solution)/shard_map/ppermute | solution.py:21
  276.3 5.2 %collective-permute-start.3 = (bf16[1,4,2056]{2,1,0:T(4,128)(2,1)S(1)}, bf16[1,4,2056]{2,1,0:T(4,128)(2,1)S(1)}, u32[]{:S(2)}, u32[]{:S(2)}) collective-permute-start(bf16[1,4,2056]{2,1,0:T(4,128)(2,1)S(1)} %get-tuple-element.56), channel_id=1, source_target_pairs={{1,0},{2,1},{3,2},{4,3},{5,4},{6,5},{7,6},{0,7},{9,8},{10,9},{11,1... | collective-permute-start | bytes 49352 | tf_op jit(solution)/shard_map/ppermute | solution.py:22
  279.1 6.4 %collective-permute-start.2 = (bf16[1,4,2056]{2,1,0:T(4,128)(2,1)S(1)}, bf16[1,4,2056]{2,1,0:T(4,128)(2,1)S(1)}, u32[]{:S(2)}, u32[]{:S(2)}) collective-permute-start(bf16[1,4,2056]{2,1,0:T(4,128)(2,1)S(1)} %get-tuple-element.55), channel_id=1, source_target_pairs={{0,1},{1,2},{2,3},{3,4},{4,5},{5,6},{6,7},{7,0},{8,9},{9,10},{10,1... | collective-permute-start | bytes 49352 | tf_op jit(solution)/shard_map/ppermute | solution.py:21
  281.6 8.9 %collective-permute-start.4 = (bf16[1,4,2056]{2,1,0:T(4,128)(2,1)S(1)}, bf16[1,4,2056]{2,1,0:T(4,128)(2,1)S(1)}, u32[]{:S(2)}, u32[]{:S(2)}) collective-permute-start(bf16[1,4,2056]{2,1,0:T(4,128)(2,1)S(1)} %get-tuple-element.57), channel_id=1, source_target_pairs={{0,1},{1,2},{2,3},{3,4},{4,5},{5,6},{6,7},{7,0},{8,9},{9,10},{10,1... | collective-permute-start | bytes 49352 | tf_op jit(solution)/shard_map/ppermute | solution.py:21
Sparse Core Ops, SparseCore 0:
  23.2 88.2 all-reduce.2
where the time goes:
time: 340 us; the launch traced here: 336 us
  local copies, waits for them, and re-layouts  152 us (45%)
  waiting for transfers between devices  85.7 us (25%)
  other arithmetic  54 us (16%)
  between operations  29.7 us (9%)
  starting transfers between devices  14.2 us (4%)
    rev x4, local copies, waits for them, and re-layouts, cut_columns(): flipped = jnp.where(flip == 1, band[..., ::-1], band)  147 us
    psum x1, waiting for transfers between devices, spread(): return lax.psum(kept, axis)  80.6 us
    another operation x2, other arithmetic, body(): deflect = jnp.stack([state[0], state[1]])[:, None]  13.4 us
    ppermute x4, starting transfers between devices, extended_2(): after = lax.ppermute(first, axis, down)  11.7 us
    another operation x4, other arithmetic, body(): distort = jnp.stack([state[2], state[3], state[4], state[5]])[:, None]  10.6 us
  transfers between devices with their start and end apart: 9, of which 4 were waited for; matrix products, arithmetic and copies ran while one was open for 20% of the time, Pallas kernels for 0%

commit v1 on v0

--- a/solution.py
+++ b/solution.py
@@ -26,7 +26,12 @@
 
 def spread(value, axis, source):
     kept = jnp.where(lax.axis_index(axis) == source, value, 0).astype(value.dtype)
-    return lax.psum(kept, axis)
+
+    def number_lane(w_in):
+        seen_now = lax.all_gather(w_in, axis_name=axis).sum(axis=0)
+        return seen_now
+
+    return number_lane(kept)
 
 
 def cubic_weights(frac):

time: 340 us -> 245 us (0.72); the launches traced: 336 us -> 245 us
  local copies, waits for them, and re-layouts: 152 us -> 46.2 us
  other arithmetic: 54 us -> 63 us
  starting transfers between devices: 14.2 us -> 20.4 us
    rev x4, local copies, waits for them, and re-layouts: 147 us -> 42.6 us  [cut_columns(): flipped = jnp.where(flip == 1, band[..., ::-1], band)]
    all_gather x0 -> x4, waiting for transfers between devices: none -> 83.5 us  [number_lane(): seen_now = lax.all_gather(w_in, axis_name=axis).sum(axis=0)]
    psum x1 -> x0, waiting for transfers between devices: 80.6 us -> none  [spread(): return lax.psum(kept, axis)]
    reduce_sum x0 -> x4, other arithmetic: none -> 11.9 us  [number_lane(): seen_now = lax.all_gather(w_in, axis_name=axis).sum(axis=0)]
    ppermute x4, starting transfers between devices: 11.7 us -> 15.7 us  [extended_2(): after = lax.ppermute(first, axis, down)]
    ppermute x4, waiting for transfers between devices: 3.65 us -> 0.01 us  [extended_2(): before = lax.ppermute(last, axis, up)]
  transfers between devices with their start and end apart: 9 -> 12, of which waited for: 4 -> 4; matrix products, arithmetic and copies ran while one was open for 20% -> 27% of each run, Pallas kernels for 0% -> 0%
where the time goes in v1:
time: 245 us
  waiting for transfers between devices  85.5 us (35%)
  other arithmetic  63 us (26%)
  local copies, waits for them, and re-layouts  46.2 us (19%)
  between operations  29.7 us (12%)
  starting transfers between devices  20.4 us (8%)
    all_gather x4, waiting for transfers between devices, number_lane(): seen_now = lax.all_gather(w_in, axis_name=axis).sum(axis=0)  83.5 us
    rev x4, local copies, waits for them, and re-layouts, cut_columns(): flipped = jnp.where(flip == 1, band[..., ::-1], band)  42.6 us
    ppermute x4, starting transfers between devices, extended_2(): after = lax.ppermute(first, axis, down)  15.7 us
    another operation x2, other arithmetic, body(): deflect = jnp.stack([state[0], state[1]])[:, None]  13.2 us
    reduce_sum x4, other arithmetic, number_lane(): seen_now = lax.all_gather(w_in, axis_name=axis).sum(axis=0)  11.9 us
    another operation x4, other arithmetic, body(): distort = jnp.stack([state[2], state[3], state[4], state[5]])[:, None]  10.1 us
    sub x1, other arithmetic, advance(): new_11 = a_11 - lens * (hess_xx * a_11 + hess_xy * a_21)  6.12 us
    add x4, other arithmetic, derivatives(): sum((first_coef[p] * first_coef[q] * window(p - 2, q - 2) for p in range(...  6 us
  transfers between devices with their start and end apart: 12, of which 4 were waited for; matrix products, arithmetic and copies ran while one was open for 27% of the time, Pallas kernels for 0%

profile of v1, /device:TPU:0, one launch (start us, length us, event | category | flops | bytes accessed | tf_op | source)
XLA Modules:
  0.0 244.7 jit_solution(12625510045282072229)
XLA Ops:
  7.2 1.5 fusion.435
  18.9 4.3 %dynamic-slice_select_fusion.3 = (bf16[1,32,16384]{2,1,0:T(8,128)(2,1)}, bf16[1,32,16384]{2,1,0:T(8,128)(2,1)}, bf16[1,32,16384]{2,1,0:T(8,128)(2,1)}, bf16[1,32,16384]{2,1,0:T(8,128)(2,1)}) fusion(bf16[2,32,16384]{2,1,0:T(8,128)(2,1)} %param.6, s32[]{:T(128)S(6)} %select_n.146, pred[]{:T(512)S(6)} %eq.49, s32[]{:T(128)S(6)} %select_n.155, pred[]{:T(512)S(6)} %eq.52, ...), kind=kLoop, calls=%fused_computation.412 | loop fusion | flops 2097152 | bytes 8388628 | tf_op jit(solution)/shard_map/jit(_where)/select_n | solution.py:28
  23.3 0.7 all-gather.11.cloned.1.call-update
  24.1 0.7 all-gather.7.cloned.1.call-update
  24.8 0.5 all-gather.5.cloned.1.call-update
  25.4 0.7 fusion.436
  28.7 0.7 fusion.434
  32.0 0.6 fusion.433
  32.7 27.9 %all-gather.9.cloned.1.call-done = bf16[4,32,16384]{2,1,0:T(8,128)(2,1)} async-done(((bf16[1,32,16384]{2,1,0:T(8,128)(2,1)}), bf16[4,32,16384]{2,1,0:T(8,128)(2,1)}) %all-gather.9.cloned.1.call-update) | async-done | bytes 4194320 | tf_op jit(solution)/shard_map/all_gather | solution.py:31
  60.6 3.0 %reduce_sum.50 = bf16[32,16384]{1,0:T(8,128)(2,1)S(1)} reduce(bf16[4,32,16384]{2,1,0:T(8,128)(2,1)} %all-gather.9.cloned.1.call-done, bf16[]{:T(256)} %constant.163.clone.1), dimensions={0}, to_apply=%region_2.3 | reduce | flops 1572864 | bytes 5242882 | tf_op jit(solution)/shard_map/reduce_sum | solution.py:31
  63.6 10.7 %rev.14 = bf16[32,16384]{1,0:T(8,128)(2,1)S(1)} reverse(bf16[32,16384]{1,0:T(8,128)(2,1)S(1)} %reduce_sum.50), dimensions={1} | reverse | bytes 2097152 | tf_op jit(solution)/shard_map/rev | solution.py:108
  74.6 1.5 collective-permute-start.4
  76.2 3.2 %collective-permute-start.5 = (bf16[1,4,2056]{2,1,0:T(4,128)(2,1)S(1)}, bf16[1,4,2056]{2,1,0:T(4,128)(2,1)S(1)}, u32[]{:S(2)}, u32[]{:S(2)}) collective-permute-start(bf16[1,4,2056]{2,1,0:T(4,128)(2,1)S(1)} %get-tuple-element.54), channel_id=1, source_target_pairs={{1,0},{2,1},{3,2},{4,3},{5,4},{6,5},{7,6},{0,7},{9,8},{10,9},{11,1... | collective-permute-start | bytes 49352 | tf_op jit(solution)/shard_map/ppermute | solution.py:22
  79.4 17.3 %all-gather.11.cloned.1.call-done = bf16[4,32,16384]{2,1,0:T(8,128)(2,1)} async-done(((bf16[1,32,16384]{2,1,0:T(8,128)(2,1)}), bf16[4,32,16384]{2,1,0:T(8,128)(2,1)}) %all-gather.11.cloned.1.call-update) | async-done | bytes 4194320 | tf_op jit(solution)/shard_map/all_gather | solution.py:31
  96.7 3.0 %reduce_sum.51 = bf16[32,16384]{1,0:T(8,128)(2,1)S(1)} reduce(bf16[4,32,16384]{2,1,0:T(8,128)(2,1)} %all-gather.11.cloned.1.call-done, bf16[]{:T(256)} %constant.163.clone.1), dimensions={0}, to_apply=%region_3.4 | reduce | flops 1572864 | bytes 5242882 | tf_op jit(solution)/shard_map/reduce_sum | solution.py:31
  99.7 10.7 %rev.15 = bf16[32,16384]{1,0:T(8,128)(2,1)S(1)} reverse(bf16[32,16384]{1,0:T(8,128)(2,1)S(1)} %reduce_sum.51), dimensions={1} | reverse | bytes 2097152 | tf_op jit(solution)/shard_map/rev | solution.py:108
  110.5 0.2 fusion.387
  110.8 1.5 collective-permute-start.6
  112.3 3.3 %collective-permute-start.7 = (bf16[1,4,2056]{2,1,0:T(4,128)(2,1)S(1)}, bf16[1,4,2056]{2,1,0:T(4,128)(2,1)S(1)}, u32[]{:S(2)}, u32[]{:S(2)}) collective-permute-start(bf16[1,4,2056]{2,1,0:T(4,128)(2,1)S(1)} %get-tuple-element.56), channel_id=1, source_target_pairs={{1,0},{2,1},{3,2},{4,3},{5,4},{6,5},{7,6},{0,7},{9,8},{10,9},{11,1... | collective-permute-start | bytes 49352 | tf_op jit(solution)/shard_map/ppermute | solution.py:22
  115.6 17.3 %all-gather.7.cloned.1.call-done = bf16[4,32,16384]{2,1,0:T(8,128)(2,1)} async-done(((bf16[1,32,16384]{2,1,0:T(8,128)(2,1)}), bf16[4,32,16384]{2,1,0:T(8,128)(2,1)}) %all-gather.7.cloned.1.call-update) | async-done | bytes 4194320 | tf_op jit(solution)/shard_map/all_gather | solution.py:31
  132.8 3.0 %reduce_sum.49 = bf16[32,16384]{1,0:T(8,128)(2,1)S(1)} reduce(bf16[4,32,16384]{2,1,0:T(8,128)(2,1)} %all-gather.7.cloned.1.call-done, bf16[]{:T(256)} %constant.163.clone.1), dimensions={0}, to_apply=%region_1.2 | reduce | flops 1572864 | bytes 5242882 | tf_op jit(solution)/shard_map/reduce_sum | solution.py:31
  135.8 10.7 %rev.13 = bf16[32,16384]{1,0:T(8,128)(2,1)S(1)} reverse(bf16[32,16384]{1,0:T(8,128)(2,1)S(1)} %reduce_sum.49), dimensions={1} | reverse | bytes 2097152 | tf_op jit(solution)/shard_map/rev | solution.py:108
  146.6 0.2 fusion.385
  146.9 1.5 collective-permute-start.2
  148.3 21.1 %all-gather.5.cloned.1.call-done = bf16[4,32,16384]{2,1,0:T(8,128)(2,1)} async-done(((bf16[1,32,16384]{2,1,0:T(8,128)(2,1)}), bf16[4,32,16384]{2,1,0:T(8,128)(2,1)}) %all-gather.5.cloned.1.call-update) | async-done | bytes 4194320 | tf_op jit(solution)/shard_map/all_gather | solution.py:31
  169.4 3.0 %reduce_sum.48 = bf16[32,16384]{1,0:T(8,128)(2,1)S(1)} reduce(bf16[4,32,16384]{2,1,0:T(8,128)(2,1)} %all-gather.5.cloned.1.call-done, bf16[]{:T(256)} %constant.163.clone.1), dimensions={0}, to_apply=%region_0.1 | reduce | flops 1572864 | bytes 5242882 | tf_op jit(solution)/shard_map/reduce_sum | solution.py:31
  172.4 10.7 %rev.12 = bf16[32,16384]{1,0:T(8,128)(2,1)S(1)} reverse(bf16[32,16384]{1,0:T(8,128)(2,1)S(1)} %reduce_sum.48), dimensions={1} | reverse | bytes 2097152 | tf_op jit(solution)/shard_map/rev | solution.py:108
  183.4 4.3 %collective-permute-start.3 = (bf16[1,4,2056]{2,1,0:T(4,128)(2,1)S(1)}, bf16[1,4,2056]{2,1,0:T(4,128)(2,1)S(1)}, u32[]{:S(2)}, u32[]{:S(2)}) collective-permute-start(bf16[1,4,2056]{2,1,0:T(4,128)(2,1)S(1)} %get-tuple-element.52), channel_id=1, source_target_pairs={{1,0},{2,1},{3,2},{4,3},{5,4},{6,5},{7,6},{0,7},{9,8},{10,9},{11,1... | collective-permute-start | bytes 49352 | tf_op jit(solution)/shard_map/ppermute | solution.py:22
  187.8 0.9 add_add_fusion.1
  188.6 1.5 fusion.15
  190.2 5.0 %collective-permute-start.1 = (bf16[1,4,2056]{2,1,0:T(4,128)(2,1)S(1)}, bf16[1,4,2056]{2,1,0:T(4,128)(2,1)S(1)}, u32[]{:S(2)}, u32[]{:S(2)}) collective-permute-start(bf16[1,4,2056]{2,1,0:T(4,128)(2,1)S(1)} %get-tuple-element.50), channel_id=1, source_target_pairs={{1,0},{2,1},{3,2},{4,3},{5,4},{6,5},{7,6},{0,7},{9,8},{10,9},{11,1... | collective-permute-start | bytes 49352 | tf_op jit(solution)/shard_map/ppermute | solution.py:22
  195.2 0.9 add_add_fusion
  196.1 1.5 fusion
  197.6 0.9 add_add_fusion.3
  198.5 1.5 fusion.30
  200.1 1.5 fusion.45
  201.6 0.9 add_add_fusion.7
  202.5 6.7 %fusion.67 = f32[1,32,2048]{2,1,0:T(8,128)S(1)} fusion(f32[35,2051]{1,0:T(8,128)S(1)} %get-tuple-element.35, f32[35,2051]{1,0:T(8,128)S(1)} %get-tuple-element.39, f32[35,2051]{1,0:T(8,128)S(1)} %get-tuple-element.43, f32[35,2051]{1,0:T(8,128)S(1)} %get-tuple-element.47, f32[]{:T(128)} %bitcast.29, f32[]{:T(128)} %bitcast.22, f32[]{:T(128)} %bitcast.15, ...), kind=kLoop, calls=%fused_computation.577 | loop fusion | flops 9633792 | bytes 17041424 | tf_op jit(solution)/shard_map/stack | solution.py:132
  209.2 6.5 %fusion.87 = f32[1,32,2048]{2,1,0:T(8,128)S(1)} fusion(f32[35,2051]{1,0:T(8,128)S(1)} %get-tuple-element.34, f32[35,2051]{1,0:T(8,128)S(1)} %get-tuple-element.38, f32[35,2051]{1,0:T(8,128)S(1)} %get-tuple-element.42, f32[35,2051]{1,0:T(8,128)S(1)} %get-tuple-element.46, f32[]{:T(128)} %bitcast.29, f32[]{:T(128)} %bitcast.22, f32[]{:T(128)} %bitcast.15, ...), kind=kLoop, calls=%fused_computation.597 | loop fusion | flops 9633792 | bytes 17041424 | tf_op jit(solution)/shard_map/stack | solution.py:132
  215.7 0.8 maximum_bitcast_fusion.1
  216.5 6.1 %multiply_subtract_fusion.9 = (f32[32,2048]{1,0:T(8,128)S(1)}, f32[32,2048]{1,0:T(8,128)S(1)}, f32[32,2048]{1,0:T(8,128)S(1)}, f32[32,2048]{1,0:T(8,128)S(1)}, f...) fusion(f32[]{:T(128)} %bitcast.15, f32[]{:T(128)} %bitcast, f32[35,2051]{1,0:T(8,128)S(1)} %get-tuple-element.44, ...), kind=kLoop, calls=%fused_computation.899 | loop fusion | flops 12320768 | bytes 22546440 | tf_op jit(solution)/shard_map/sub | solution.py:100
  222.7 2.9 %multiply_subtract_fusion.8 = (f32[32,2048]{1,0:T(8,128)S(1)}, f32[32,2048]{1,0:T(8,128)S(1)}) fusion(f32[32,2048]{1,0:T(8,128)S(1)} %get-tuple-element.20, f32[]{:T(128)} %bitcast.15, f32[32,2048]{1,0:T(8,128)S(1)} %get-tuple-element.18, f32[32,2048]{1,0:T(8,128)S(1)} %get-tuple-element.19, f32[]{:T(128)} %bitcast, f32[32,2048]{1,0:T(8,128)S(1)} %get-tuple-element.17, ...), kind=kLoop, calls=%fused_computation.898 | loop fusion | flops 3145728 | bytes 5769224 | tf_op jit(solution)/shard_map/sub | solution.py:102
  225.5 1.5 multiply_subtract_fusion.2
  227.0 6.0 %subtract_bitcast_fusion.3 = (f32[1,32,2048]{2,1,0:T(8,128)S(1)}, f32[32,2048]{1,0:T(8,128)S(1)}, f32[32,2048]{1,0:T(8,128)S(1)}, f32[32,2048]{1,0:T(8,128)S(1)}...) fusion(f32[]{:T(128)} %bitcast.29, ...), kind=kLoop, calls=%fused_computation.895 | loop fusion | flops 12451840 | bytes 23595016 | tf_op jit(solution)/shard_map/stack | solution.py:133
  233.0 2.1 subtract_bitcast_fusion.1
  235.1 1.3 subtract_bitcast_fusion.2
  236.5 0.6 subtract_bitcast_fusion
  237.1 1.0 maximum_bitcast_fusion
  (42 shorter events, 1.5 us)
Async XLA Ops:
  7.2 53.4 %all-gather.9.cloned.1.call-start = ((), (), s32[]{:S(2)}) async-start(), calls=%async_computation.2 | async-start | bytes 5242880 | tf_op jit(solution)/shard_map/all_gather | solution.py:31
  23.3 73.5 %all-gather.11.cloned.1.call-start = ((), (), s32[]{:S(2)}) async-start(), calls=%async_computation.3 | async-start | bytes 5242880 | tf_op jit(solution)/shard_map/all_gather | solution.py:31
  24.0 1.4 copy-start
  24.0 4.7 %copy-start.1 = (s32[1,4]{1,0:T(1,128)S(1)}, s32[1,4]{1,0:T(1,128)}, u32[]{:S(2)}) copy-start(s32[1,4]{1,0:T(1,128)} %param.9) | copy-start | bytes 52
  24.0 8.0 %copy-start.2 = (f32[4]{0:T(128)S(1)}, f32[4]{0:T(128)}, u32[]{:S(2)}) copy-start(f32[4]{0:T(128)} %param.11) | copy-start | bytes 52
  24.0 8.6 %copy-start.3 = (s32[4,16]{1,0:T(4,128)S(1)}, s32[4,16]{1,0:T(4,128)}, u32[]{:S(2)}) copy-start(s32[4,16]{1,0:T(4,128)} %param.10) | copy-start | bytes 772
  24.1 108.8 %all-gather.7.cloned.1.call-start = ((), (), s32[]{:S(2)}) async-start(), calls=%async_computation.1 | async-start | bytes 5242880 | tf_op jit(solution)/shard_map/all_gather | solution.py:31
  24.8 144.6 %all-gather.5.cloned.1.call-start = ((), (), s32[]{:S(2)}) async-start(), calls=%async_computation | async-start | bytes 5242880 | tf_op jit(solution)/shard_map/all_gather | solution.py:31
  74.6 108.8 %collective-permute-start.4 = (bf16[1,4,2056]{2,1,0:T(4,128)(2,1)S(1)}, bf16[1,4,2056]{2,1,0:T(4,128)(2,1)S(1)}, u32[]{:S(2)}, u32[]{:S(2)}) collective-permute-start(bf16[1,4,2056]{2,1,0:T(4,128)(2,1)S(1)} %get-tuple-element.53), channel_id=1, source_target_pairs={{0,1},{1,2},{2,3},{3,4},{4,5},{5,6},{6,7},{7,0},{8,9},{9,10},{10,1... | collective-permute-start | bytes 49352 | tf_op jit(solution)/shard_map/ppermute | solution.py:21
  76.2 111.5 %collective-permute-start.5 = (bf16[1,4,2056]{2,1,0:T(4,128)(2,1)S(1)}, bf16[1,4,2056]{2,1,0:T(4,128)(2,1)S(1)}, u32[]{:S(2)}, u32[]{:S(2)}) collective-permute-start(bf16[1,4,2056]{2,1,0:T(4,128)(2,1)S(1)} %get-tuple-element.54), channel_id=1, source_target_pairs={{1,0},{2,1},{3,2},{4,3},{5,4},{6,5},{7,6},{0,7},{9,8},{10,9},{11,1... | collective-permute-start | bytes 49352 | tf_op jit(solution)/shard_map/ppermute | solution.py:22
  110.8 79.4 %collective-permute-start.6 = (bf16[1,4,2056]{2,1,0:T(4,128)(2,1)S(1)}, bf16[1,4,2056]{2,1,0:T(4,128)(2,1)S(1)}, u32[]{:S(2)}, u32[]{:S(2)}) collective-permute-start(bf16[1,4,2056]{2,1,0:T(4,128)(2,1)S(1)} %get-tuple-element.55), channel_id=1, source_target_pairs={{0,1},{1,2},{2,3},{3,4},{4,5},{5,6},{6,7},{7,0},{8,9},{9,10},{10,1... | collective-permute-start | bytes 49352 | tf_op jit(solution)/shard_map/ppermute | solution.py:21
  112.3 82.8 %collective-permute-start.7 = (bf16[1,4,2056]{2,1,0:T(4,128)(2,1)S(1)}, bf16[1,4,2056]{2,1,0:T(4,128)(2,1)S(1)}, u32[]{:S(2)}, u32[]{:S(2)}) collective-permute-start(bf16[1,4,2056]{2,1,0:T(4,128)(2,1)S(1)} %get-tuple-element.56), channel_id=1, source_target_pairs={{1,0},{2,1},{3,2},{4,3},{5,4},{6,5},{7,6},{0,7},{9,8},{10,9},{11,1... | collective-permute-start | bytes 49352 | tf_op jit(solution)/shard_map/ppermute | solution.py:22
  146.9 50.7 %collective-permute-start.2 = (bf16[1,4,2056]{2,1,0:T(4,128)(2,1)S(1)}, bf16[1,4,2056]{2,1,0:T(4,128)(2,1)S(1)}, u32[]{:S(2)}, u32[]{:S(2)}) collective-permute-start(bf16[1,4,2056]{2,1,0:T(4,128)(2,1)S(1)} %get-tuple-element.51), channel_id=1, source_target_pairs={{0,1},{1,2},{2,3},{3,4},{4,5},{5,6},{6,7},{7,0},{8,9},{9,10},{10,1... | collective-permute-start | bytes 49352 | tf_op jit(solution)/shard_map/ppermute | solution.py:21
  183.4 14.1 %collective-permute-start.3 = (bf16[1,4,2056]{2,1,0:T(4,128)(2,1)S(1)}, bf16[1,4,2056]{2,1,0:T(4,128)(2,1)S(1)}, u32[]{:S(2)}, u32[]{:S(2)}) collective-permute-start(bf16[1,4,2056]{2,1,0:T(4,128)(2,1)S(1)} %get-tuple-element.52), channel_id=1, source_target_pairs={{1,0},{2,1},{3,2},{4,3},{5,4},{6,5},{7,6},{0,7},{9,8},{10,9},{11,1... | collective-permute-start | bytes 49352 | tf_op jit(solution)/shard_map/ppermute | solution.py:22
  187.7 12.3 %collective-permute-start = (bf16[1,4,2056]{2,1,0:T(4,128)(2,1)S(1)}, bf16[1,4,2056]{2,1,0:T(4,128)(2,1)S(1)}, u32[]{:S(2)}, u32[]{:S(2)}) collective-permute-start(bf16[1,4,2056]{2,1,0:T(4,128)(2,1)S(1)} %get-tuple-element.49), channel_id=1, source_target_pairs={{0,1},{1,2},{2,3},{3,4},{4,5},{5,6},{6,7},{7,0},{8,9},{9,10},{10,1... | collective-permute-start | bytes 49352 | tf_op jit(solution)/shard_map/ppermute | solution.py:21
  190.2 9.9 %collective-permute-start.1 = (bf16[1,4,2056]{2,1,0:T(4,128)(2,1)S(1)}, bf16[1,4,2056]{2,1,0:T(4,128)(2,1)S(1)}, u32[]{:S(2)}, u32[]{:S(2)}) collective-permute-start(bf16[1,4,2056]{2,1,0:T(4,128)(2,1)S(1)} %get-tuple-element.50), channel_id=1, source_target_pairs={{1,0},{2,1},{3,2},{4,3},{5,4},{6,5},{7,6},{0,7},{9,8},{10,9},{11,1... | collective-permute-start | bytes 49352 | tf_op jit(solution)/shard_map/ppermute | solution.py:22
Sparse Core Ops, SparseCore 0:
  23.4 37.1 all-gather.8
  62.2 34.5 all-gather.10
  98.3 34.4 all-gather.6
  134.8 34.5 all-gather.4
